TPU v7x, 32 devices: a whole 2x2x4 slice. The times are simulated.
32 devices in a mesh: groups: 2 (over y), wide: 16 (over z, x, core).
Axes of the slice: x: 2, y: 2, z: 4, core: 2. Of those that a mesh axis runs over, the one named last changes fastest.
Arguments:
- fields: bfloat16 [32, 512], P(('groups', 'wide')), parts along dimension 0, may hold values from -6 to 6
- chol: bfloat16 [512, 1024, 1024], P(None, 'wide'), may hold values from -0.01171875 to 0.01171875
- orbitals: bfloat16 [32, 1024, 256], P(('groups', 'wide')), parts along dimension 0, may hold values from -6 to 6
- trial: bfloat16 [1024, 256], replicated, may hold values from -0.5 to 0.5
Outputs:
- new_orbitals: bfloat16 [32, 1024, 256], P(('groups', 'wide')), parts along dimension 0
- force_bias: float32 [32, 2, 512], P(('groups', 'wide')), parts along dimension 0
There are 2 independent parts, one for each index of `groups`. A program takes and returns all parts, laid end to end along the dimension named above; an argument that names none is the same for every part. Nothing has to cross between parts.
All inputs are finite; a program needn't handle non-finite values.
Results may differ from a plain program's by a relative error of at most 0.0075.
Values may be sent and summed in bfloat16 or wider, within the bound.
No kernel may reach another device: no remote copies, remote signals or barrier semaphores. Data moves between devices by JAX's collectives and lax.ppermute only.
A program may use at most 192 MiB of HBM per device.

v0:
```python
import jax
import jax.numpy as jnp
from jax import lax
from jax.sharding import PartitionSpec as P

TAYLOR = 4


def per_device(fields, chol, orbitals, trial):
    all_fields = lax.all_gather(fields, "wide", axis=0, tiled=True)
    vectors, rows, width = chol.shape
    chol_flat = chol.reshape(vectors, rows * width)
    generator = jnp.dot(all_fields, chol_flat, preferred_element_type=jnp.float32).astype(
        jnp.bfloat16
    )
    generator = generator.reshape(all_fields.shape[0], rows, width)
    owned = lax.all_to_all(generator, "wide", split_axis=0, concat_axis=1, tiled=True)
    nocc = orbitals.shape[2] // 2
    walk_local = orbitals.shape[0]
    gen_walker = owned[0]
    total = orbitals[0].astype(jnp.float32)
    operand = orbitals[0]
    for order in range(1, TAYLOR + 1):
        product = jnp.dot(gen_walker, operand, preferred_element_type=jnp.float32)
        term = jnp.concatenate([-product[:, nocc:], product[:, :nocc]], axis=1) / order
        total = total + term
        if order < TAYLOR:
            operand = term.astype(jnp.bfloat16)
    fresh_list = [total.astype(jnp.bfloat16)]
    new_orbitals = jnp.stack(fresh_list, axis=0)
    trial_real = trial[:, :nocc].T
    trial_imag = trial[:, nocc:].T
    mixer = jnp.concatenate(
        [
            jnp.concatenate([trial_real, -trial_imag], axis=1),
            jnp.concatenate([trial_imag, trial_real], axis=1),
        ],
        axis=0,
    )
    orbital_rows = lax.all_to_all(new_orbitals, "wide", split_axis=1, concat_axis=0, tiled=True)
    count = orbital_rows.shape[0]
    flat_rows = orbital_rows.reshape(count * rows, 2 * nocc)
    tile_green = jnp.dot(flat_rows, mixer, preferred_element_type=jnp.float32).astype(jnp.bfloat16)
    tile_green = tile_green.reshape(count, rows, 2 * width)
    all_walk = tile_green.shape[0]
    tile_green = (
        tile_green.reshape(all_walk, rows, 2, width)
        .transpose(0, 2, 1, 3)
        .reshape(all_walk * 2, rows * width)
    )
    partial_value = jnp.dot(tile_green, chol_flat.T, preferred_element_type=jnp.float32).reshape(
        all_walk, 2, vectors
    )
    summed = lax.psum(partial_value, "wide")
    force_bias = lax.dynamic_slice_in_dim(
        summed, lax.axis_index("wide") * walk_local, walk_local, 0
    )
    return (new_orbitals, force_bias)


def solution(mesh):
    in_specs = (
        P(("groups", "wide"), None),
        P(None, "wide", None),
        P(("groups", "wide"), None, None),
        P(),
    )
    out_specs = (P(("groups", "wide"), None, None), P(("groups", "wide"), None, None))
    return jax.shard_map(
        per_device, mesh=mesh, in_specs=in_specs, out_specs=out_specs, check_vma=False
    )
```

profile of v0, /device:TPU:8, one launch (start us, length us, event | category | flops | bytes accessed | tf_op | source)
XLA Modules:
  0.0 381.3 jit_solution(17390543338026890626)
XLA Ops:
  7.2 58.5 %copy.31 = bf16[64,8,64,1024]{3,1,2,0:T(8,128)(2,1)} copy(bf16[64,8,64,1024]{3,2,1,0:T(8,128)(2,1)} %bitcast.19) | data formatting | bytes 134217728
  65.7 18.9 %all-gather = bf16[16,1,512]{2,1,0:T(2,128)(2,1)S(1)} all-gather(bf16[1,1,512]{2,1,0:T(2,128)(2,1)S(1)} %bitcast.65), channel_id=1, replica_groups=mesh['groups'=2,'wide'=16] {'wide'}, dimensions={0}, use_global_device_ids=true | all-gather | bytes 17408 | tf_op jit(solution)/shard_map/all_gather | solution.py:10
  84.6 22.8 %convolution_convert_fusion = bf16[16,65536]{1,0:T(8,128)(2,1)S(1)} fusion(bf16[512,65536]{1,0:T(8,128)(2,1)} %bitcast.20, bf16[16,1,512]{2,1,0:T(2,128)(2,1)S(1)} %all-gather), kind=kOutput, calls=%fused_computation | convolution fusion | flops 1074790400 | bytes 69222400 | tf_op jit(solution)/shard_map/dot_general | solution.py:13
  107.4 2.5 copy.32
  109.9 6.9 %all-to-all-start = ((bf16[16,64,1024]{2,1,0:T(8,128)(2,1)}), bf16[16,64,1024]{2,1,0:T(8,128)(2,1)S(1)}, u32[]{:S(2)}, u32[]{:S(2)}) async-start(bf16[16,64,1024]{2,1,0:T(8,128)(2,1)} %bitcast.62), calls=%async_computation | async-start | bytes 4194304 | tf_op jit(solution)/shard_map/all_to_all | solution.py:17
  116.8 0.2 copy.22
  117.0 45.6 %all-to-all-done = bf16[16,64,1024]{2,1,0:T(8,128)(2,1)S(1)} async-done(((bf16[16,64,1024]{2,1,0:T(8,128)(2,1)}), bf16[16,64,1024]{2,1,0:T(8,128)(2,1)S(1)}, u32[]{:S(2)}, u32[]{:S(2)}) %all-to-all-start) | async-done | bytes 2097184 | tf_op jit(solution)/shard_map/all_to_all | solution.py:17
  162.7 0.8 fusion.34
  163.4 0.1 fusion.38
  163.6 0.7 fusion.28
  164.3 0.1 slice_negate_fusion.2
  164.5 0.7 fusion.25
  165.2 0.1 slice_negate_fusion.1
  165.4 0.7 fusion.23
  166.1 0.1 fusion.27
  166.2 0.6 fusion.13
  166.8 0.9 copy.23
  167.7 0.5 broadcast.24
  168.2 3.8 %reduce = bf16[1024,256]{1,0:T(8,128)(2,1)S(1)} reduce(bf16[1024,1,256]{2,1,0:T(2,128)(2,1)S(1)} %bitcast.63, bf16[]{:T(256)} %broadcast.24), dimensions={1}, to_apply=%bitcast.50.reduce_sub_computation | reduce | bytes 1048578
  172.0 0.9 reshape.121
  172.9 6.4 %all-to-all-start.1 = ((bf16[16,2,8192]{2,1,0:T(2,128)(2,1)}), bf16[16,2,8192]{2,1,0:T(2,128)(2,1)S(1)}, u32[]{:S(2)}, u32[]{:S(2)}) async-start(bf16[16,2,8192]{2,1,0:T(2,128)(2,1)} %reshape.121), calls=%async_computation.1 | async-start | bytes 1048576 | tf_op jit(solution)/shard_map/all_to_all | solution.py:40
  179.3 0.0 all-reduce.2.cloned.1.call-start
  179.4 13.3 %all-to-all-done.1 = bf16[16,2,8192]{2,1,0:T(2,128)(2,1)S(1)} async-done(((bf16[16,2,8192]{2,1,0:T(2,128)(2,1)}), bf16[16,2,8192]{2,1,0:T(2,128)(2,1)S(1)}, u32[]{:S(2)}, u32[]{:S(2)}) %all-to-all-start.1) | async-done | bytes 524320 | tf_op jit(solution)/shard_map/all_to_all | solution.py:40
  192.8 0.5 reshape.122
  193.3 3.3 convolution_convert_fusion.1
  196.6 7.8 %reshape_reshape.3 = bf16[16,64,2,1024]{3,2,1,0:T(2,128)(2,1)} reshape(bf16[1024,2048]{1,0:T(8,128)(2,1)} %convolution_convert_fusion.1) | data formatting | bytes 8388608 | tf_op jit(solution)/shard_map/reshape;reshape | solution.py:47
  204.3 80.0 %fusion.5 = f32[16,2,512]{2,0,1:T(8,128)} fusion(bf16[512,64,1024]{2,1,0:T(8,128)(2,1)} %param.5, bf16[16,64,2,1024]{3,2,1,0:T(2,128)(2,1)} %reshape_reshape.3), kind=kOutput, calls=%fused_computation.7 | convolution fusion | flops 2147483648 | bytes 71368704 | tf_op jit(solution)/shard_map/dot_general | solution.py:51
  284.3 0.0 all-reduce.2.cloned.1.call-update
  284.3 1.0 copy.26
  285.3 87.8 %all-reduce.2.cloned.1.call-done = f32[16,2,512]{2,0,1:T(8,128)} async-done(((f32[16,2,512]{2,0,1:T(8,128)}), f32[16,2,512]{2,0,1:T(8,128)}) %all-reduce.2.cloned.1.call-update) | async-done | bytes 65552 | tf_op jit(solution)/shard_map/psum | solution.py:54
  373.1 0.8 constant_dynamic-slice_fusion
  373.9 0.6 copy.27
  (9 shorter events, 0.1 us)
Async XLA Ops:
  7.2 58.6 %copy-start.2 = (bf16[1,512]{1,0:T(2,128)(2,1)S(1)}, bf16[1,512]{1,0:T(2,128)(2,1)}, u32[]{:S(2)}) copy-start(bf16[1,512]{1,0:T(2,128)(2,1)} %param.4) | copy-start | bytes 3076
  109.9 6.9 %copy-start = (bf16[1,1024,256]{2,1,0:T(8,128)(2,1)S(1)}, bf16[1,1024,256]{2,1,0:T(8,128)(2,1)}, u32[]{:S(2)}) copy-start(bf16[1,1024,256]{2,1,0:T(8,128)(2,1)} %param.6) | copy-start | bytes 1572868
  109.9 52.8 %all-to-all-start = ((bf16[16,64,1024]{2,1,0:T(8,128)(2,1)}), bf16[16,64,1024]{2,1,0:T(8,128)(2,1)S(1)}, u32[]{:S(2)}, u32[]{:S(2)}) async-start(bf16[16,64,1024]{2,1,0:T(8,128)(2,1)} %bitcast.62), calls=%async_computation | async-start | bytes 4194304 | tf_op jit(solution)/shard_map/all_to_all | solution.py:17
  167.6 11.7 %copy-start.1 = (bf16[1024,256]{1,0:T(8,128)(2,1)S(1)}, bf16[1024,256]{1,0:T(8,128)(2,1)}, u32[]{:S(2)}) copy-start(bf16[1024,256]{1,0:T(8,128)(2,1)} %param.7) | copy-start | bytes 1572868
  172.9 19.8 %all-to-all-start.1 = ((bf16[16,2,8192]{2,1,0:T(2,128)(2,1)}), bf16[16,2,8192]{2,1,0:T(2,128)(2,1)S(1)}, u32[]{:S(2)}, u32[]{:S(2)}) async-start(bf16[16,2,8192]{2,1,0:T(2,128)(2,1)} %reshape.121), calls=%async_computation.1 | async-start | bytes 1048576 | tf_op jit(solution)/shard_map/all_to_all | solution.py:40
  179.3 193.8 %all-reduce.2.cloned.1.call-start = ((), (), s32[]{:S(2)}) async-start(), calls=%async_computation.2 | async-start | bytes 131072 | tf_op jit(solution)/shard_map/psum | solution.py:54
Sparse Core Ops, SparseCore 0:
  284.4 88.6 all-reduce.1
where the time goes:
time: 382 us; the launch traced here: 381 us
  waiting for transfers between devices  147 us (38%)
  matrix products  109 us (29%)
  local copies, waits for them, and re-layouts  74.3 us (19%)
  blocking collectives  18.9 us (5%)
  between operations  14.2 us (4%)
  starting transfers between devices  13.3 us (3%)
  other arithmetic  4.9 us (1%)
    psum x1, waiting for transfers between devices, per_device(): summed = lax.psum(partial_value, 'wide')  87.8 us
    dot_general x1, matrix products, per_device(): jnp.dot(tile_green, chol_flat.T, preferred_element_type=jnp.float32)  80 us
    unnamed x14, local copies, waits for them, and re-layouts  64.8 us
    all_to_all x1, waiting for transfers between devices, per_device(): lax.all_to_all(generator, 'wide', split_axis=0, concat_axis=1, tiled=True)  45.6 us
    dot_general x1, matrix products, per_device(): jnp.dot(all_fields, chol_flat, preferred_element_type=jnp.float32)  22.8 us
    all_gather x1, blocking collectives, per_device(): all_fields = lax.all_gather(fields, 'wide', axis=0, tiled=True)  18.9 us
    all_to_all x1, waiting for transfers between devices, per_device(): lax.all_to_all(new_orbitals, 'wide', split_axis=1, concat_axis=0, tiled=T...  13.3 us
    another operation x1, local copies, waits for them, and re-layouts, per_device(): tile_green.reshape(all_walk, rows, 2, width).transpose(0, 2, 1, 3)  7.78 us
  transfers between devices with their start and end apart: 3, of which 3 were waited for; matrix products, arithmetic and copies ran while one was open for 0% of the time, Pallas kernels for 0%

commit v1 on v0

--- a/solution.py
+++ b/solution.py
@@ -4,6 +4,15 @@
 from jax.sharding import PartitionSpec as P
 
 TAYLOR = 4
+
+
+def spread_masks(state):
+    mesh_dim = "wide"
+    degree = lax.axis_size(mesh_dim)
+    odd = state
+    for rr in [t for t in (1, 2, 4, 8, 16) if t < degree]:
+        odd = odd + lax.ppermute(odd, mesh_dim, tuple(((i0, i0 ^ rr) for i0 in range(degree))))
+    return odd
 
 
 def per_device(fields, chol, orbitals, trial):
@@ -51,7 +60,7 @@
     partial_value = jnp.dot(tile_green, chol_flat.T, preferred_element_type=jnp.float32).reshape(
         all_walk, 2, vectors
     )
-    summed = lax.psum(partial_value, "wide")
+    summed = spread_masks(partial_value)
     force_bias = lax.dynamic_slice_in_dim(
         summed, lax.axis_index("wide") * walk_local, walk_local, 0
     )

time: 382 us -> 295 us (0.77)
  waiting for transfers between devices: 147 us -> 70.5 us
  between operations: 14.2 us -> 0.81 us
    psum x1 -> x0, waiting for transfers between devices: 87.8 us -> none  [per_device(): summed = lax.psum(partial_value, 'wide')]
    ppermute x0 -> x4, waiting for transfers between devices: none -> 11.5 us  [spread_masks(): lax.ppermute(odd, mesh_dim, tuple(((i0, i0 ^ rr) for i0 in range(degree))))]
  transfers between devices with their start and end apart: 3 -> 6, of which waited for: 3 -> 6; matrix products, arithmetic and copies ran while one was open for 0% -> 0% of each run, Pallas kernels for 0% -> 0%
where the time goes in v1:
time: 295 us; the launch traced here: 294 us
  matrix products  108 us (37%)
  local copies, waits for them, and re-layouts  73.5 us (25%)
  waiting for transfers between devices  70.5 us (24%)
  blocking collectives  18.9 us (6%)
  starting transfers between devices  16.5 us (6%)
  other arithmetic  4.98 us (2%)
    dot_general x1, matrix products, per_device(): jnp.dot(tile_green, chol_flat.T, preferred_element_type=jnp.float32)  79.4 us
    unnamed x14, local copies, waits for them, and re-layouts  64.8 us
    all_to_all x1, waiting for transfers between devices, per_device(): lax.all_to_all(generator, 'wide', split_axis=0, concat_axis=1, tiled=True)  45.6 us
    dot_general x1, matrix products, per_device(): jnp.dot(all_fields, chol_flat, preferred_element_type=jnp.float32)  22.8 us
    all_gather x1, blocking collectives, per_device(): all_fields = lax.all_gather(fields, 'wide', axis=0, tiled=True)  18.9 us
    all_to_all x1, waiting for transfers between devices, per_device(): lax.all_to_all(new_orbitals, 'wide', split_axis=1, concat_axis=0, tiled=T...  13.4 us
    ppermute x4, waiting for transfers between devices, spread_masks(): lax.ppermute(odd, mesh_dim, tuple(((i0, i0 ^ rr) for i0 in range(degree))))  11.5 us
    another operation x1, local copies, waits for them, and re-layouts, per_device(): tile_green.reshape(all_walk, rows, 2, width).transpose(0, 2, 1, 3)  7.83 us
  transfers between devices with their start and end apart: 6, of which 6 were waited for; matrix products, arithmetic and copies ran while one was open for 0% of the time, Pallas kernels for 0%

profile of v1, /device:TPU:8, one launch (start us, length us, event | category | flops | bytes accessed | tf_op | source)
XLA Modules:
  0.0 293.5 jit_solution(1017835121993209400)
XLA Ops:
  0.6 58.5 %copy.31 = bf16[64,8,64,1024]{3,1,2,0:T(8,128)(2,1)} copy(bf16[64,8,64,1024]{3,2,1,0:T(8,128)(2,1)} %bitcast.19) | data formatting | bytes 134217728
  59.2 18.9 %all-gather = bf16[16,1,512]{2,1,0:T(2,128)(2,1)S(1)} all-gather(bf16[1,1,512]{2,1,0:T(2,128)(2,1)S(1)} %bitcast.65), channel_id=1, replica_groups=mesh['groups'=2,'wide'=16] {'wide'}, dimensions={0}, use_global_device_ids=true | all-gather | bytes 17408 | tf_op jit(solution)/shard_map/all_gather | solution.py:19
  78.1 22.8 %convolution_convert_fusion = bf16[16,65536]{1,0:T(8,128)(2,1)S(1)} fusion(bf16[512,65536]{1,0:T(8,128)(2,1)} %bitcast.20, bf16[16,1,512]{2,1,0:T(2,128)(2,1)S(1)} %all-gather), kind=kOutput, calls=%fused_computation | convolution fusion | flops 1074790400 | bytes 69222400 | tf_op jit(solution)/shard_map/dot_general | solution.py:22
  100.8 2.5 copy.32
  103.3 6.9 %all-to-all-start = ((bf16[16,64,1024]{2,1,0:T(8,128)(2,1)}), bf16[16,64,1024]{2,1,0:T(8,128)(2,1)S(1)}, u32[]{:S(2)}, u32[]{:S(2)}) async-start(bf16[16,64,1024]{2,1,0:T(8,128)(2,1)} %bitcast.62), calls=%async_computation | async-start | bytes 4194304 | tf_op jit(solution)/shard_map/all_to_all | solution.py:26
  110.2 0.2 copy.22
  110.5 45.6 %all-to-all-done = bf16[16,64,1024]{2,1,0:T(8,128)(2,1)S(1)} async-done(((bf16[16,64,1024]{2,1,0:T(8,128)(2,1)}), bf16[16,64,1024]{2,1,0:T(8,128)(2,1)S(1)}, u32[]{:S(2)}, u32[]{:S(2)}) %all-to-all-start) | async-done | bytes 2097184 | tf_op jit(solution)/shard_map/all_to_all | solution.py:26
  156.1 0.7 fusion.34
  157.0 0.7 fusion.28
  157.9 0.7 fusion.25
  158.8 0.7 fusion.23
  159.7 0.6 fusion.13
  160.2 0.9 copy.23
  161.1 0.5 broadcast.24
  161.6 3.8 %reduce = bf16[1024,256]{1,0:T(8,128)(2,1)S(1)} reduce(bf16[1024,1,256]{2,1,0:T(2,128)(2,1)S(1)} %bitcast.63, bf16[]{:T(256)} %broadcast.24), dimensions={1}, to_apply=%bitcast.50.reduce_sub_computation | reduce | bytes 1048578
  165.5 0.9 reshape.121
  166.4 6.4 %all-to-all-start.1 = ((bf16[16,2,8192]{2,1,0:T(2,128)(2,1)}), bf16[16,2,8192]{2,1,0:T(2,128)(2,1)S(1)}, u32[]{:S(2)}, u32[]{:S(2)}) async-start(bf16[16,2,8192]{2,1,0:T(2,128)(2,1)} %reshape.121), calls=%async_computation.1 | async-start | bytes 1048576 | tf_op jit(solution)/shard_map/all_to_all | solution.py:49
  172.9 13.4 %all-to-all-done.1 = bf16[16,2,8192]{2,1,0:T(2,128)(2,1)S(1)} async-done(((bf16[16,2,8192]{2,1,0:T(2,128)(2,1)}), bf16[16,2,8192]{2,1,0:T(2,128)(2,1)S(1)}, u32[]{:S(2)}, u32[]{:S(2)}) %all-to-all-start.1) | async-done | bytes 524320 | tf_op jit(solution)/shard_map/all_to_all | solution.py:49
  186.2 0.5 reshape.122
  186.8 3.2 %convolution_convert_fusion.1 = bf16[1024,2048]{1,0:T(8,128)(2,1)} fusion(bf16[128,1024]{0,1:T(8,128)(2,1)S(1)} %get-tuple-element.24, bf16[128,1024]{0,1:T(8,128)(2,1)S(1)} %get-tuple-element.23, bf16[128,1024]{0,1:T(8,128)(2,1)S(1)} %fusion.48, bf16[1,1024,256]{2,0,1:T(2,128)(2,1)S(1)} %bitcast.64), kind=kOutput, calls=%fused_computation.6 | convolution fusion | flops 1080033280 | bytes 5505024 | tf_op jit(solution)/shard_map/dot_general | solution.py:52
  190.0 7.8 %reshape_reshape.3 = bf16[16,64,2,1024]{3,2,1,0:T(2,128)(2,1)} reshape(bf16[1024,2048]{1,0:T(8,128)(2,1)} %convolution_convert_fusion.1) | data formatting | bytes 8388608 | tf_op jit(solution)/shard_map/reshape;reshape | solution.py:56
  197.8 79.4 %fusion.5 = f32[16,2,512]{2,0,1:T(8,128)S(1)} fusion(bf16[512,64,1024]{2,1,0:T(8,128)(2,1)} %param.5, bf16[16,64,2,1024]{3,2,1,0:T(2,128)(2,1)} %reshape_reshape.3), kind=kOutput, calls=%fused_computation.7 | convolution fusion | flops 2147483648 | bytes 71368704 | tf_op jit(solution)/shard_map/dot_general | solution.py:60
  277.2 0.8 collective-permute-start
  278.0 0.9 collective-permute-done
  278.9 1.0 collective-permute-start.1
  279.9 3.4 %collective-permute-done.1 = f32[16,2,512]{2,0,1:T(8,128)S(1)} collective-permute-done((f32[16,2,512]{2,0,1:T(8,128)S(1)}, f32[16,2,512]{2,0,1:T(8,128)S(1)}, u32[]{:S(2)}, u32[]{:S(2)}) %collective-permute-start.1) | collective-permute-done | bytes 65568 | tf_op jit(solution)/shard_map/ppermute | solution.py:14
  283.4 0.5 collective-permute-start.2
  283.8 3.9 %collective-permute-done.2 = f32[16,2,512]{2,0,1:T(8,128)S(1)} collective-permute-done((f32[16,2,512]{2,0,1:T(8,128)S(1)}, f32[16,2,512]{2,0,1:T(8,128)S(1)}, u32[]{:S(2)}, u32[]{:S(2)}) %collective-permute-start.2) | collective-permute-done | bytes 65568 | tf_op jit(solution)/shard_map/ppermute | solution.py:14
  287.7 0.9 collective-permute-start.3
  288.6 1.0 copy.26
  289.6 3.3 %collective-permute-done.3 = f32[16,2,512]{2,0,1:T(8,128)S(1)} collective-permute-done((f32[16,2,512]{2,0,1:T(8,128)S(1)}, f32[16,2,512]{2,0,1:T(8,128)S(1)}, u32[]{:S(2)}, u32[]{:S(2)}) %collective-permute-start.3) | collective-permute-done | bytes 65568 | tf_op jit(solution)/shard_map/ppermute | solution.py:14
  292.9 0.6 copy.27
  (17 shorter events, 0.7 us)
Async XLA Ops:
  0.6 58.6 %copy-start.2 = (bf16[1,512]{1,0:T(2,128)(2,1)S(1)}, bf16[1,512]{1,0:T(2,128)(2,1)}, u32[]{:S(2)}) copy-start(bf16[1,512]{1,0:T(2,128)(2,1)} %param.4) | copy-start | bytes 3076
  103.3 6.9 %copy-start = (bf16[1,1024,256]{2,1,0:T(8,128)(2,1)S(1)}, bf16[1,1024,256]{2,1,0:T(8,128)(2,1)}, u32[]{:S(2)}) copy-start(bf16[1,1024,256]{2,1,0:T(8,128)(2,1)} %param.6) | copy-start | bytes 1572868
  103.3 52.8 %all-to-all-start = ((bf16[16,64,1024]{2,1,0:T(8,128)(2,1)}), bf16[16,64,1024]{2,1,0:T(8,128)(2,1)S(1)}, u32[]{:S(2)}, u32[]{:S(2)}) async-start(bf16[16,64,1024]{2,1,0:T(8,128)(2,1)} %bitcast.62), calls=%async_computation | async-start | bytes 4194304 | tf_op jit(solution)/shard_map/all_to_all | solution.py:26
  161.1 11.6 %copy-start.1 = (bf16[1024,256]{1,0:T(8,128)(2,1)S(1)}, bf16[1024,256]{1,0:T(8,128)(2,1)}, u32[]{:S(2)}) copy-start(bf16[1024,256]{1,0:T(8,128)(2,1)} %param.7) | copy-start | bytes 1572868
  166.4 19.9 %all-to-all-start.1 = ((bf16[16,2,8192]{2,1,0:T(2,128)(2,1)}), bf16[16,2,8192]{2,1,0:T(2,128)(2,1)S(1)}, u32[]{:S(2)}, u32[]{:S(2)}) async-start(bf16[16,2,8192]{2,1,0:T(2,128)(2,1)} %reshape.121), calls=%async_computation.1 | async-start | bytes 1048576 | tf_op jit(solution)/shard_map/all_to_all | solution.py:49
  277.2 1.7 collective-permute-start
  278.9 4.4 %collective-permute-start.1 = (f32[16,2,512]{2,0,1:T(8,128)S(1)}, f32[16,2,512]{2,0,1:T(8,128)S(1)}, u32[]{:S(2)}, u32[]{:S(2)}) collective-permute-start(f32[16,2,512]{2,0,1:T(8,128)S(1)} %add.35), channel_id=1, source_target_pairs={{0,2},{1,3},{2,0},{3,1},{4,6},{5,7},{6,4},{7,5},{8,10},{9,11},{10,... | collective-permute-start | bytes 196616 | tf_op jit(solution)/shard_map/ppermute | solution.py:14
  283.4 4.3 %collective-permute-start.2 = (f32[16,2,512]{2,0,1:T(8,128)S(1)}, f32[16,2,512]{2,0,1:T(8,128)S(1)}, u32[]{:S(2)}, u32[]{:S(2)}) collective-permute-start(f32[16,2,512]{2,0,1:T(8,128)S(1)} %add.36), channel_id=1, source_target_pairs={{0,4},{1,5},{2,6},{3,7},{4,0},{5,1},{6,2},{7,3},{8,12},{9,13},{10,... | collective-permute-start | bytes 196616 | tf_op jit(solution)/shard_map/ppermute | solution.py:14
  287.7 5.2 %collective-permute-start.3 = (f32[16,2,512]{2,0,1:T(8,128)S(1)}, f32[16,2,512]{2,0,1:T(8,128)S(1)}, u32[]{:S(2)}, u32[]{:S(2)}) collective-permute-start(f32[16,2,512]{2,0,1:T(8,128)S(1)} %add.37), channel_id=1, source_target_pairs={{0,8},{1,9},{2,10},{3,11},{4,12},{5,13},{6,14},{7,15},{8,0},{9,1},... | collective-permute-start | bytes 196616 | tf_op jit(solution)/shard_map/ppermute | solution.py:14
